TPU v7x, 512 devices: a whole 4x4x16 slice. The times are simulated.
512 devices in a mesh: dp: 4 (over y), expert: 32 (over z, core), tensor: 4 (over x).
Axes of the slice: x: 4, y: 4, z: 16, core: 2. Of those that a mesh axis runs over, the one named last changes fastest.
Arguments:
- tokens: bfloat16 [16384, 2048], P(('dp', 'expert')), may hold values from -6 to 6
- cotangent: bfloat16 [16384, 2048], P(('dp', 'expert')), may hold values from -6 to 6
- expert_ids: int32 [16384, 1], P(('dp', 'expert')), may hold values from 0 to 31; in each aligned block of 128 rows (0 to 127, 128 to 255, ...) at most 8 rows name the same one
- gate_weight: bfloat16 [32, 2048, 1408], P('expert', 'dp', 'tensor'), may hold values from -0.125 to 0.125
- up_weight: bfloat16 [32, 2048, 1408], P('expert', 'dp', 'tensor'), may hold values from -0.125 to 0.125
- down_weight: bfloat16 [32, 2048, 1408], P('expert', 'dp', 'tensor'), may hold values from -0.15625 to 0.15625
Outputs:
- grad_tokens: bfloat16 [16384, 2048], P(('dp', 'expert'), 'tensor')
- grad_gate: bfloat16 [32, 2048, 1408], P('expert', 'dp', 'tensor')
- grad_up: bfloat16 [32, 2048, 1408], P('expert', 'dp', 'tensor')
Inputs may be any that keep to these rules, and one draw needn't show every extreme that they name: `expert_ids`: among the 128 tokens of one block no expert id occurs more than 8 times, and in every draw some block holds some id exactly 8 times.
All inputs are finite; a program needn't handle non-finite values.
Results may differ from a plain program's by a relative error of at most 0.013.
Values may be sent and summed in bfloat16 or wider, within the bound.
A program may use at most 64 MiB of HBM per device.

v0:
```python
import functools

import jax
import jax.numpy as jnp
from jax import lax
from jax.experimental import pallas as pl
from jax.experimental.pallas import tpu as pltpu
from jax.sharding import PartitionSpec as P

CAP = 8
CORES = 2
LAG = 4
F32 = jnp.float32
BF16 = jnp.bfloat16
MESH = pl.DeviceIdType.MESH


def nt(a, b):
    return lax.dot_general(a, b, (((1,), (1,)), ((), ())), preferred_element_type=F32)


def nn(a, b):
    return lax.dot_general(a, b, (((1,), (0,)), ((), ())), preferred_element_type=F32)


def tn(a, b):
    return lax.dot_general(a, b, (((0,), (0,)), ((), ())), preferred_element_type=F32)


def kernel(
    sizes,
    ids_hbm, tokens_hbm, cotangent_hbm, gate_hbm, up_hbm, down_hbm,
    out_rows, out_gate, out_up,
    ids, mine, sbuf, afull, wfull, placer, acc, gact, tfull, wsum, pbuf, x1, x2, rbuf, back,
    ins, zs, zr, xg_s, xg_r, xh_s, xh_r, ws, wr, vs, vr, bs, br, p1_s, p1_r, p2_s, p2_r,
    as_s, as_r, ah_s, ah_r, e_s, e_r, f1_s, f1_r, f2_s, f2_r, known,
):
    n_dp, n_expert, n_tensor = sizes
    i, e, t = lax.axis_index("dp"), lax.axis_index("expert"), lax.axis_index("tensor")
    z, core = lax.div(e, CORES), lax.rem(e, CORES)
    chips = n_expert // CORES
    half_ring = chips // 2
    block, features = tokens_hbm.shape
    part = features // n_tensor
    width = part // n_dp
    rows = n_expert * CAP
    hidden = gate_hbm.shape[0]
    half_hidden = hidden // 2
    weights = (down_hbm, gate_hbm, up_hbm)
    i_left, i_opp, i_right = (lax.rem(i + k, n_dp) for k in (n_dp - 1, 2, 1))
    t_left, t_opp, t_right = (lax.rem(t + k, n_tensor) for k in (n_tensor - 1, 2, 1))
    y_peer = ({"dp": i_left}, {"dp": i_right})
    x_peer = ({"tensor": t_left}, {"tensor": t_right})
    TO_LEFT, TO_RIGHT = 0, 1

    def copy(src, dst, send, recv, peer):
        return pltpu.make_async_remote_copy(
            src_ref=src, dst_ref=dst, send_sem=send, recv_sem=recv, device_id=peer, device_id_type=MESH
        )

    barrier = pltpu.get_barrier_semaphore()
    other = z * CORES + 1 - core
    z_next, z_prev = lax.rem(z + 1, chips), lax.rem(z + chips - 1, chips)
    near = y_peer + x_peer + ({"dp": i_opp}, {"expert": other})
    near += tuple({"expert": chip * CORES + c} for chip in (z_prev, z_next) for c in range(CORES))
    z_peer = ({"expert": z_prev * CORES + core}, {"expert": z_next * CORES + core})
    for peer in near:
        pl.semaphore_signal(barrier, inc=1, device_id=peer, device_id_type=MESH)

    fetch_rows = [pltpu.make_async_copy(ids_hbm, ids, ins.at[0])]
    for kind, array in enumerate((tokens_hbm, cotangent_hbm)):
        for j in range(n_dp):
            columns = pl.ds(pl.multiple_of(j * part + t * width, width), width)
            fetch_rows.append(
                pltpu.make_async_copy(
                    array.at[:, columns], mine.at[kind, :, pl.ds(j * width, width)], ins.at[1 + kind * n_dp + j]
                )
            )
    fetch_weights = [pltpu.make_async_copy(weights[k], wfull.at[k, 3], ins.at[1 + 2 * n_dp + k]) for k in range(3)]
    for fetch in fetch_rows + fetch_weights:
        fetch.start()

    def weight_first(k, d):
        return copy(weights[k], wfull.at[k, 2 if d == TO_LEFT else 0], ws.at[k, d], wr.at[k, d], y_peer[d])

    def weight_second(k, d):
        cut = pl.ds(0 if d == TO_RIGHT else half_hidden, half_hidden)
        return copy(
            wfull.at[k, 0 if d == TO_RIGHT else 2, cut], wfull.at[k, 1, cut], vs.at[k, d], vr.at[k, d], y_peer[d]
        )

    def weight_forward(k):
        for d in range(2):
            weight_first(k, d).wait_recv()
            weight_second(k, d).start()

    pl.semaphore_wait(barrier, len(near))
    for k in range(3):
        for d in range(2):
            weight_first(k, d).start()

    def report(d):
        pl.semaphore_signal(known.at[d], inc=1, device_id=z_peer[d], device_id_type=MESH)

    report(0)
    report(1)

    for fetch in fetch_rows:
        fetch.wait()
    chosen = ids[...]
    onehot = (lax.broadcasted_iota(jnp.int32, (n_expert, block), 0) == chosen).astype(BF16)
    before = (
        lax.broadcasted_iota(jnp.int32, (block, block), 0) < lax.broadcasted_iota(jnp.int32, (block, block), 1)
    ).astype(BF16)
    earlier = nn(onehot, before)
    position = jnp.sum(earlier * onehot.astype(F32), axis=0, keepdims=True).astype(jnp.int32)
    target = chosen * CAP + position
    placer[...] = (lax.broadcasted_iota(jnp.int32, (rows, block), 0) == target).astype(BF16)
    for kind in range(2):
        sbuf[:, pl.ds(kind * part, part)] = nn(placer[...], mine[kind]).astype(BF16)

    def eight(k):
        return pl.ds(pl.multiple_of(k * CAP, CAP), CAP)

    def both(k):
        return pl.ds(pl.multiple_of(k * (CORES * CAP), CORES * CAP), CORES * CAP)

    def expert_at(away, c):
        return lax.rem(z + away, chips) * CORES + c

    def back_from(away):
        return lax.rem(chips - away, chips)

    def dispatch(away, c):
        to, place = expert_at(away, c), back_from(away) * CORES + core
        return copy(
            sbuf.at[eight(to)], afull.at[t, eight(place)], zs.at[away * CORES + c], zr.at[place], {"expert": to}
        )

    def arrived(away, c):
        place = away * CORES + c
        copy(
            sbuf.at[eight(other)], afull.at[t, eight(place)], zs.at[place], zr.at[place], {"expert": other}
        ).wait_recv()

    def send_to(away):
        for c in range(CORES):
            dispatch(away, c).start()

    dispatch(0, 1 - core).start()
    own = pltpu.make_async_copy(sbuf.at[eight(e)], afull.at[t, eight(core)], zs.at[core])
    own.start()
    send_to(1)
    send_to(chips - 1)

    def send_further(m, carry):
        for d in range(2):
            pl.semaphore_wait(known.at[d], 1)
            report(d)
        send_to(m + 1)
        send_to(chips - m - 1)
        return carry

    lax.fori_loop(1, half_ring - 1, send_further, 0)
    for d in range(2):
        pl.semaphore_wait(known.at[d], 1)
    send_to(half_ring)

    def chunk(m):
        odd = lax.rem(m, 2)
        return lax.rem(odd * (chips - lax.div(m + 1, 2)) + (1 - odd) * lax.div(m, 2), chips)

    def spread_first(q, m, d):
        c = both(chunk(m))
        return copy(afull.at[q, c], afull.at[q, c], xg_s.at[d, m], xg_r.at[d, m], x_peer[d])

    def spread_second(q, m, d):
        c = eight(chunk(m) * CORES + (0 if d == TO_RIGHT else 1))
        return copy(afull.at[q, c], afull.at[q, c], xh_s.at[d, m], xh_r.at[d, m], x_peer[d])

    def spread_own(m):
        for d in range(2):
            spread_first(t, m, d).start()

    def forward(m):
        for d in range(2):
            from_q = t_left if d == TO_RIGHT else t_right
            spread_first(from_q, m, d).wait_recv()
            spread_second(from_q, m, d).start()

    def take(m, carry):
        for c in range(CORES):
            arrived(chunk(m), c)
        spread_own(m)
        return carry

    def take_and_forward(m, carry):
        take(m, carry)
        forward(m - LAG)
        return carry

    def forward_only(m, carry):
        forward(m)
        return carry

    own.wait()
    arrived(0, 1 - core)
    spread_own(0)
    lax.fori_loop(1, LAG, take, 0)
    lax.fori_loop(LAG, 11, take_and_forward, 0)
    weight_forward(0)
    lax.fori_loop(11, 15, take_and_forward, 0)
    weight_forward(1)
    lax.fori_loop(15, chips, take_and_forward, 0)
    lax.fori_loop(chips - LAG, chips, forward_only, 0)
    weight_forward(2)

    def exchange(r):
        j = lax.rem(i + r, n_dp)
        columns = pl.ds(pl.multiple_of(j * width, width), width)
        return copy(afull.at[t, :, columns], tfull.at[t, r - 1], e_s.at[r - 1], e_r.at[r - 1], {"dp": j})

    for r in range(1, n_dp):
        exchange(r).start()

    def finish_rows(m, carry):
        for d in range(2):
            spread_second(t_opp, m, d).wait_recv()
        return carry

    lax.fori_loop(0, chips, finish_rows, 0)
    for fetch in fetch_weights:
        fetch.wait()

    def rows_of(j, kind):
        columns = pl.ds(pl.multiple_of(kind * part + j * width, width), width)
        return jnp.concatenate([afull[q, :, columns] for q in range(n_tensor)], axis=1)

    for k, kind in enumerate((1, 0, 0)):
        acc[k] = nt(wfull[k, 3], rows_of(i, kind))
        acc[k] += nt(wfull[k, 0], rows_of(i_left, kind))
        acc[k] += nt(wfull[k, 2], rows_of(i_right, kind))
        for d in range(2):
            weight_second(k, d).wait_recv()
        acc[k] += nt(wfull[k, 1], rows_of(i_opp, kind))

    hidden_grad, gate_act, up_act = acc[0], acc[1], acc[2]
    sigmoid_gate = jax.nn.sigmoid(gate_act)
    scaled = hidden_grad * sigmoid_gate
    gact[3, 0] = (scaled * up_act * (1.0 + gate_act * (1.0 - sigmoid_gate))).astype(BF16)
    gact[3, 1] = (scaled * gate_act).astype(BF16)

    def act_first(d):
        return copy(gact.at[3], gact.at[2 if d == TO_LEFT else 0], as_s.at[d], as_r.at[d], y_peer[d])

    def act_second(d):
        k = 0 if d == TO_RIGHT else 1
        return copy(gact.at[0 if d == TO_RIGHT else 2, k], gact.at[1, k], ah_s.at[d], ah_r.at[d], y_peer[d])

    for d in range(2):
        act_first(d).start()

    def input_term(r):
        q = lax.rem(t + r, n_tensor)
        slot = 3 - lax.rem(q + n_dp - i, n_dp)
        pbuf[r] = (tn(gact[3, 0], wfull[1, slot]) + tn(gact[3, 1], wfull[2, slot])).astype(BF16)

    piece = rows // 4
    cuts = ((pl.ds(piece, piece), pl.ds(2 * piece, piece)), (pl.ds(0, piece), pl.ds(3 * piece, piece)))

    def part_hop(d, far):
        cut = cuts[far][0 if d == TO_RIGHT else 1]
        return copy(pbuf.at[2, cut], x1.at[d, far], p1_s.at[d, far], p1_r.at[d, far], x_peer[d])

    def part_last(d, far, h):
        cut = cuts[far][h]
        r = 1 if d == TO_RIGHT else 3
        return copy(pbuf.at[r, cut], x2.at[d, cut], p2_s.at[d, far, h], p2_r.at[d, far, h], x_peer[d])

    def relay(far):
        for d, r, h in ((TO_RIGHT, 1, 0), (TO_LEFT, 3, 1)):
            cut = cuts[far][h]
            part_hop(d, far).wait_recv()
            pbuf[r, cut] = (pbuf[r, cut].astype(F32) + x1[d, far].astype(F32)).astype(BF16)
            part_last(d, far, h).start()

    def own_half(far):
        part_last(TO_RIGHT, far, 1).start()
        part_last(TO_LEFT, far, 0).start()

    input_term(2)
    for far in range(2):
        for d in range(2):
            part_hop(d, far).start()
    input_term(1)
    input_term(3)
    own_half(0)
    relay(0)
    own_half(1)
    relay(1)
    input_term(0)

    def share_first(d):
        return copy(tfull.at[t], tfull.at[t], f1_s.at[d], f1_r.at[d], x_peer[d])

    def share_second(q, d):
        cut = pl.ds(0 if d == TO_RIGHT else rows // 2, rows // 2)
        return copy(tfull.at[q, :, cut], tfull.at[q, :, cut], f2_s.at[d], f2_r.at[d], x_peer[d])

    for r in range(1, n_dp):
        exchange(r).wait_recv()
    for d in range(2):
        share_first(d).start()

    def give_back(away, c):
        place = away * CORES + c
        to = expert_at(away, c)
        return copy(
            rbuf.at[eight(place)], back.at[eight(e)], bs.at[place], br.at[back_from(away) * CORES + core], {"expert": to}
        )

    def add_up(far):
        for h in range(2):
            cut = cuts[far][h]
            for d in range(2):
                part_last(d, far, h).wait_recv()
            total = pbuf[0, cut].astype(F32) + x2[0, cut].astype(F32) + x2[1, cut].astype(F32)
            rbuf[cut, :] = total.astype(BF16)

    def give(m, carry):
        for c in range(CORES):
            give_back(half_ring + m, c).start()
            give_back(half_ring - 1 - m, c).start()
        return carry

    quarter_ring = half_ring // 2
    add_up(0)
    lax.fori_loop(0, quarter_ring, give, 0)
    for d in range(2):
        act_first(d).wait_recv()
        act_second(d).start()
    add_up(1)
    lax.fori_loop(quarter_ring, half_ring - 1, give, 0)
    for c in range(CORES):
        give_back(chips - 1, c).start()
    give_back(0, 1 - core).start()
    kept = pltpu.make_async_copy(rbuf.at[eight(core)], back.at[eight(e)], bs.at[core])
    kept.start()
    for d in range(2):
        share_first(d).wait_recv()
        share_second(t_left if d == TO_RIGHT else t_right, d).start()

    for k in range(2):
        wsum[k] = nn(gact[3, k], rows_of(i, 0))
    for d in range(2):
        share_second(t_opp, d).wait_recv()

    def group_rows(r):
        return jnp.concatenate([tfull[q, r - 1] for q in range(n_tensor)], axis=1)

    for k in range(2):
        wsum[k] += nn(gact[0, k], group_rows(1)) + nn(gact[2, k], group_rows(3))
    for d in range(2):
        act_second(d).wait_recv()
    for k, out in enumerate((out_gate, out_up)):
        out[...] = (wsum[k] + nn(gact[1, k], group_rows(2))).astype(BF16)

    def returned(away, c):
        place = away * CORES + c
        source = expert_at(away, c)
        copy(rbuf.at[eight(place)], back.at[eight(source)], bs.at[place], br.at[place], {"expert": other}).wait_recv()

    def take_back(away, carry):
        for c in range(CORES):
            returned(away, c)
        return carry

    kept.wait()
    returned(0, 1 - core)
    lax.fori_loop(1, chips, take_back, 0)
    out_rows[...] = tn(placer[...], back[...]).astype(BF16)

    dispatch(0, 1 - core).wait_send()
    give_back(0, 1 - core).wait_send()

    def sent(away, carry):
        for c in range(CORES):
            dispatch(away, c).wait_send()
            give_back(away, c).wait_send()
        return carry

    lax.fori_loop(1, chips, sent, 0)

    def spread_sent(m, carry):
        for d in range(2):
            spread_first(t, m, d).wait_send()
            spread_second(t_left if d == TO_RIGHT else t_right, m, d).wait_send()
        return carry

    lax.fori_loop(0, chips, spread_sent, 0)
    for r in range(1, n_dp):
        exchange(r).wait_send()
    for d in range(2):
        act_first(d).wait_send()
        act_second(d).wait_send()
        share_first(d).wait_send()
        share_second(t_left if d == TO_RIGHT else t_right, d).wait_send()
        for far in range(2):
            part_hop(d, far).wait_send()
            for h in range(2):
                part_last(d, far, h).wait_send()
        for k in range(3):
            weight_first(k, d).wait_send()
            weight_second(k, d).wait_send()


def on_device(sizes, tokens, cotangent, expert_ids, gate_weight, up_weight, down_weight):
    n_dp, n_expert, n_tensor = sizes
    block, features = tokens.shape
    hidden, depth = gate_weight.shape[2], gate_weight.shape[1]
    part, rows, chips = features // n_tensor, n_expert * CAP, n_expert // CORES
    dma = pltpu.SemaphoreType.DMA
    flip = lambda w: jnp.swapaxes(w, 1, 2)[0]
    operands = (expert_ids.reshape(1, block), tokens, cotangent, flip(gate_weight), flip(up_weight), flip(down_weight))
    grad_rows, grad_gate, grad_up = pl.pallas_call(
        functools.partial(kernel, sizes),
        out_shape=(
            jax.ShapeDtypeStruct((block, part), BF16),
            jax.ShapeDtypeStruct((hidden, depth), BF16),
            jax.ShapeDtypeStruct((hidden, depth), BF16),
        ),
        in_specs=[pl.BlockSpec(memory_space=pltpu.HBM)] * 6,
        out_specs=[pl.BlockSpec(memory_space=pltpu.VMEM)] * 3,
        scratch_shapes=[
            pltpu.VMEM((1, block), jnp.int32),
            pltpu.VMEM((2, block, part), BF16),
            pltpu.VMEM((rows, 2 * part), BF16),
            pltpu.VMEM((n_tensor, rows, 2 * part), BF16),
            pltpu.VMEM((3, n_dp, hidden, depth), BF16),
            pltpu.VMEM((rows, block), BF16),
            pltpu.VMEM((3, hidden, rows), F32),
            pltpu.VMEM((n_dp, 2, hidden, rows), BF16),
            pltpu.VMEM((n_tensor, n_dp - 1, rows, part // n_dp), BF16),
            pltpu.VMEM((2, hidden, depth), F32),
            pltpu.VMEM((n_tensor, rows, part), BF16),
            pltpu.VMEM((2, 2, rows // 4, part), BF16),
            pltpu.VMEM((2, rows, part), BF16),
            pltpu.VMEM((rows, part), BF16),
            pltpu.VMEM((rows, part), BF16),
            dma((1 + 2 * n_dp + 3,)), dma((n_expert,)), dma((n_expert,)),
            dma((2, chips)), dma((2, chips)), dma((2, chips)), dma((2, chips)),
            dma((3, 2)), dma((3, 2)), dma((3, 2)), dma((3, 2)),
            dma((n_expert,)), dma((n_expert,)),
            dma((2, 2)), dma((2, 2)), dma((2, 2, 2)), dma((2, 2, 2)),
            dma((2,)), dma((2,)), dma((2,)), dma((2,)),
            dma((n_dp - 1,)), dma((n_dp - 1,)),
            dma((2,)), dma((2,)), dma((2,)), dma((2,)),
            pltpu.SemaphoreType.REGULAR((2,)),
        ],
        compiler_params=pltpu.CompilerParams(
            collective_id=0, has_side_effects=True, vmem_limit_bytes=48 << 20
        ),
        name="moe_backward",
    )(*(pltpu.with_memory_space_constraint(a, pltpu.HBM) for a in operands))
    back = lambda g: jnp.swapaxes(g[None], 1, 2)
    return grad_rows, back(grad_gate), back(grad_up)


def solution(mesh):
    sizes = tuple(mesh.shape[a] for a in ("dp", "expert", "tensor"))
    row, weight = P(("dp", "expert"), None), P("expert", "dp", "tensor")
    return jax.shard_map(
        functools.partial(on_device, sizes),
        mesh=mesh,
        in_specs=(row, row, row, weight, weight, weight),
        out_specs=(P(("dp", "expert"), "tensor"), weight, weight),
        check_vma=False,
    )
```

profile of v0, /device:TPU:1, one launch (start us, length us, event | category | flops | bytes accessed | tf_op | source)
XLA Modules:
  0.0 81.9 jit_solution(16440197744559853020)
XLA Ops:
  0.6 79.1 %moe_backward.1 = (bf16[128,512]{1,0:T(8,128)(2,1)S(1)}, bf16[352,512]{1,0:T(8,128)(2,1)S(1)}, bf16[352,512]{1,0:T(8,128)(2,1)S(1)}) custom-call(s32[1,128]{1,0:T(1,128)} %bitcast.21, bf16[128,2048]{1,0:T(8,128)(2,1)} %tokens_hbm.1, bf16[128,2048]{1,0:T(8,128)(2,1)} %cotangent_hbm.1, bf16[352,512]{1,0:T(8,128)(2,1)} %bitcast.18, bf16[352,512]{1,0:T(8,128)(2,1)} %bitcast.19, ...), custom_call_target="tpu_custom_call" | custom-call | tf_op jit(solution)/shard_map/moe_backward/pallas_call | solution.py:425
  79.8 0.7 copy.12
  80.4 0.7 copy.13
  81.1 0.7 copy.14
where the time goes:
time: 82 us; the launch traced here: 81.9 us
  Pallas kernels  79.1 us (96%)
  local copies, waits for them, and re-layouts  2.13 us (3%)
    pallas_call x1, Pallas kernels, on_device(): pl.pallas_call(functools.partial(kernel, sizes), out_shape=(jax.ShapeDtyp...  79.1 us
    unnamed x3, local copies, waits for them, and re-layouts  2.13 us

commit v1 on v0

--- a/solution.py
+++ b/solution.py
@@ -10,6 +10,8 @@
 CAP = 8
 CORES = 2
 LAG = 4
+EARLY = 4
+PIECES = 4
 F32 = jnp.float32
 BF16 = jnp.bfloat16
 MESH = pl.DeviceIdType.MESH
@@ -46,7 +48,7 @@
     rows = n_expert * CAP
     hidden = gate_hbm.shape[0]
     half_hidden = hidden // 2
-    weights = (down_hbm, gate_hbm, up_hbm)
+    weights = (gate_hbm, up_hbm, down_hbm)
     i_left, i_opp, i_right = (lax.rem(i + k, n_dp) for k in (n_dp - 1, 2, 1))
     t_left, t_opp, t_right = (lax.rem(t + k, n_tensor) for k in (n_tensor - 1, 2, 1))
     y_peer = ({"dp": i_left}, {"dp": i_right})
@@ -128,19 +130,13 @@
     def expert_at(away, c):
         return lax.rem(z + away, chips) * CORES + c
 
-    def back_from(away):
-        return lax.rem(chips - away, chips)
-
     def dispatch(away, c):
-        to, place = expert_at(away, c), back_from(away) * CORES + core
-        return copy(
-            sbuf.at[eight(to)], afull.at[t, eight(place)], zs.at[away * CORES + c], zr.at[place], {"expert": to}
-        )
-
-    def arrived(away, c):
-        place = away * CORES + c
+        to = expert_at(away, c)
+        return copy(sbuf.at[eight(to)], afull.at[t, eight(e)], zs.at[to], zr.at[e], {"expert": to})
+
+    def arrived(source):
         copy(
-            sbuf.at[eight(other)], afull.at[t, eight(place)], zs.at[place], zr.at[place], {"expert": other}
+            sbuf.at[eight(other)], afull.at[t, eight(source)], zs.at[source], zr.at[source], {"expert": other}
         ).wait_recv()
 
     def send_to(away):
@@ -148,7 +144,7 @@
             dispatch(away, c).start()
 
     dispatch(0, 1 - core).start()
-    own = pltpu.make_async_copy(sbuf.at[eight(e)], afull.at[t, eight(core)], zs.at[core])
+    own = pltpu.make_async_copy(sbuf.at[eight(e)], afull.at[t, eight(e)], zs.at[e])
     own.start()
     send_to(1)
     send_to(chips - 1)
@@ -168,7 +164,7 @@
 
     def chunk(m):
         odd = lax.rem(m, 2)
-        return lax.rem(odd * (chips - lax.div(m + 1, 2)) + (1 - odd) * lax.div(m, 2), chips)
+        return lax.rem(z + odd * (chips - lax.div(m + 1, 2)) + (1 - odd) * lax.div(m, 2), chips)
 
     def spread_first(q, m, d):
         c = both(chunk(m))
@@ -190,7 +186,7 @@
 
     def take(m, carry):
         for c in range(CORES):
-            arrived(chunk(m), c)
+            arrived(chunk(m) * CORES + c)
         spread_own(m)
         return carry
 
@@ -203,8 +199,38 @@
         forward(m)
         return carry
 
+    def exchange(r):
+        j = lax.rem(i + r, n_dp)
+        columns = pl.ds(pl.multiple_of(j * width, width), width)
+        return copy(afull.at[t, :, columns], tfull.at[t, r - 1], e_s.at[r - 1], e_r.at[r - 1], {"dp": j})
+
+    def share_first(d):
+        return copy(tfull.at[t], tfull.at[t], f1_s.at[d], f1_r.at[d], x_peer[d])
+
+    def share_second(q, d):
+        cut = pl.ds(0 if d == TO_RIGHT else rows // 2, rows // 2)
+        return copy(tfull.at[q, :, cut], tfull.at[q, :, cut], f2_s.at[d], f2_r.at[d], x_peer[d])
+
+    def exchange_start():
+        for r in range(1, n_dp):
+            exchange(r).start()
+
+    def share_start():
+        for r in range(1, n_dp):
+            exchange(r).wait_recv()
+        for d in range(2):
+            share_first(d).start()
+
+    def share_forward():
+        for d in range(2):
+            share_first(d).wait_recv()
+            share_second(t_left if d == TO_RIGHT else t_right, d).start()
+
+    early = z < chips // EARLY
+    late = z >= chips // EARLY
+
     own.wait()
-    arrived(0, 1 - core)
+    arrived(other)
     spread_own(0)
     lax.fori_loop(1, LAG, take, 0)
     lax.fori_loop(LAG, 11, take_and_forward, 0)
@@ -212,16 +238,10 @@
     lax.fori_loop(11, 15, take_and_forward, 0)
     weight_forward(1)
     lax.fori_loop(15, chips, take_and_forward, 0)
+    pl.when(early)(exchange_start)
     lax.fori_loop(chips - LAG, chips, forward_only, 0)
     weight_forward(2)
-
-    def exchange(r):
-        j = lax.rem(i + r, n_dp)
-        columns = pl.ds(pl.multiple_of(j * width, width), width)
-        return copy(afull.at[t, :, columns], tfull.at[t, r - 1], e_s.at[r - 1], e_r.at[r - 1], {"dp": j})
-
-    for r in range(1, n_dp):
-        exchange(r).start()
+    pl.when(late)(exchange_start)
 
     def finish_rows(m, carry):
         for d in range(2):
@@ -229,6 +249,7 @@
         return carry
 
     lax.fori_loop(0, chips, finish_rows, 0)
+    pl.when(early)(share_start)
     for fetch in fetch_weights:
         fetch.wait()
 
@@ -236,119 +257,130 @@
         columns = pl.ds(pl.multiple_of(kind * part + j * width, width), width)
         return jnp.concatenate([afull[q, :, columns] for q in range(n_tensor)], axis=1)
 
-    for k, kind in enumerate((1, 0, 0)):
+    def product(k, kind):
         acc[k] = nt(wfull[k, 3], rows_of(i, kind))
         acc[k] += nt(wfull[k, 0], rows_of(i_left, kind))
         acc[k] += nt(wfull[k, 2], rows_of(i_right, kind))
+
+    def product_end(k, kind):
         for d in range(2):
             weight_second(k, d).wait_recv()
-        acc[k] += nt(wfull[k, 1], rows_of(i_opp, kind))
-
-    hidden_grad, gate_act, up_act = acc[0], acc[1], acc[2]
+        return acc[k] + nt(wfull[k, 1], rows_of(i_opp, kind))
+
+    for k, kind in enumerate((0, 0, 1)):
+        product(k, kind)
+    gate_act = product_end(0, 0)
     sigmoid_gate = jax.nn.sigmoid(gate_act)
-    scaled = hidden_grad * sigmoid_gate
-    gact[3, 0] = (scaled * up_act * (1.0 + gate_act * (1.0 - sigmoid_gate))).astype(BF16)
-    gact[3, 1] = (scaled * gate_act).astype(BF16)
-
-    def act_first(d):
-        return copy(gact.at[3], gact.at[2 if d == TO_LEFT else 0], as_s.at[d], as_r.at[d], y_peer[d])
-
-    def act_second(d):
-        k = 0 if d == TO_RIGHT else 1
-        return copy(gact.at[0 if d == TO_RIGHT else 2, k], gact.at[1, k], ah_s.at[d], ah_r.at[d], y_peer[d])
-
-    for d in range(2):
-        act_first(d).start()
+    acc[0] = gate_act * sigmoid_gate
+    acc[1] = product_end(1, 0) * (sigmoid_gate * (1.0 + gate_act * (1.0 - sigmoid_gate)))
+    hidden_grad = product_end(2, 1)
+    gact[3, 0] = (hidden_grad * acc[1]).astype(BF16)
+    gact[3, 1] = (hidden_grad * acc[0]).astype(BF16)
+
+    def act_first(k, d):
+        return copy(gact.at[3, k], gact.at[2 if d == TO_LEFT else 0, k], as_s.at[k, d], as_r.at[k, d], y_peer[d])
+
+    def act_second(k, d):
+        cut = pl.ds(0 if d == TO_RIGHT else half_hidden, half_hidden)
+        return copy(
+            gact.at[0 if d == TO_RIGHT else 2, k, cut], gact.at[1, k, cut], ah_s.at[k, d], ah_r.at[k, d], y_peer[d]
+        )
+
+    def act_forward(k):
+        for d in range(2):
+            act_first(k, d).wait_recv()
+            act_second(k, d).start()
+
+    for k in range(2):
+        for d in range(2):
+            act_first(k, d).start()
 
     def input_term(r):
         q = lax.rem(t + r, n_tensor)
         slot = 3 - lax.rem(q + n_dp - i, n_dp)
-        pbuf[r] = (tn(gact[3, 0], wfull[1, slot]) + tn(gact[3, 1], wfull[2, slot])).astype(BF16)
-
-    piece = rows // 4
-    cuts = ((pl.ds(piece, piece), pl.ds(2 * piece, piece)), (pl.ds(0, piece), pl.ds(3 * piece, piece)))
-
-    def part_hop(d, far):
-        cut = cuts[far][0 if d == TO_RIGHT else 1]
-        return copy(pbuf.at[2, cut], x1.at[d, far], p1_s.at[d, far], p1_r.at[d, far], x_peer[d])
-
-    def part_last(d, far, h):
-        cut = cuts[far][h]
+        pbuf[r] = (tn(gact[3, 0], wfull[0, slot]) + tn(gact[3, 1], wfull[1, slot])).astype(BF16)
+
+    size = rows // 2 // PIECES
+    cuts = [[pl.ds(h * rows // 2 + p * size, size) for h in range(2)] for p in range(PIECES)]
+
+    def part_hop(d, p):
+        cut = cuts[p][0 if d == TO_RIGHT else 1]
+        return copy(pbuf.at[2, cut], x1.at[d, p], p1_s.at[d, p], p1_r.at[d, p], x_peer[d])
+
+    def part_last(d, p, h):
+        cut = cuts[p][h]
         r = 1 if d == TO_RIGHT else 3
-        return copy(pbuf.at[r, cut], x2.at[d, cut], p2_s.at[d, far, h], p2_r.at[d, far, h], x_peer[d])
-
-    def relay(far):
+        return copy(pbuf.at[r, cut], x2.at[d, cut], p2_s.at[d, p, h], p2_r.at[d, p, h], x_peer[d])
+
+    def hop(p):
+        for d in range(2):
+            part_hop(d, p).start()
+
+    def relay(p):
         for d, r, h in ((TO_RIGHT, 1, 0), (TO_LEFT, 3, 1)):
-            cut = cuts[far][h]
-            part_hop(d, far).wait_recv()
-            pbuf[r, cut] = (pbuf[r, cut].astype(F32) + x1[d, far].astype(F32)).astype(BF16)
-            part_last(d, far, h).start()
-
-    def own_half(far):
-        part_last(TO_RIGHT, far, 1).start()
-        part_last(TO_LEFT, far, 0).start()
+            cut = cuts[p][h]
+            part_hop(d, p).wait_recv()
+            pbuf[r, cut] = (pbuf[r, cut].astype(F32) + x1[d, p].astype(F32)).astype(BF16)
+            part_last(d, p, h).start()
+
+    def own_half(p):
+        part_last(TO_RIGHT, p, 1).start()
+        part_last(TO_LEFT, p, 0).start()
+
+    def give_back(to):
+        return copy(rbuf.at[eight(to)], back.at[eight(e)], bs.at[to], br.at[e], {"expert": to})
+
+    def add_up(p):
+        for h in range(2):
+            cut = cuts[p][h]
+            for d in range(2):
+                part_last(d, p, h).wait_recv()
+            total = pbuf[0, cut].astype(F32) + x2[0, cut].astype(F32) + x2[1, cut].astype(F32)
+            rbuf[cut, :] = total.astype(BF16)
+
+    def give(place):
+        for h in range(2):
+            to = h * (n_expert // 2) + place
+
+            @pl.when(to != e)
+            def _():
+                give_back(to).start()
+
+    def give_piece(p):
+        for place in range(p * n_expert // 2 // PIECES, (p + 1) * n_expert // 2 // PIECES):
+            give(place)
 
     input_term(2)
-    for far in range(2):
-        for d in range(2):
-            part_hop(d, far).start()
+    hop(0)
+    hop(1)
     input_term(1)
     input_term(3)
     own_half(0)
     relay(0)
+    hop(2)
     own_half(1)
+    input_term(0)
     relay(1)
-    input_term(0)
-
-    def share_first(d):
-        return copy(tfull.at[t], tfull.at[t], f1_s.at[d], f1_r.at[d], x_peer[d])
-
-    def share_second(q, d):
-        cut = pl.ds(0 if d == TO_RIGHT else rows // 2, rows // 2)
-        return copy(tfull.at[q, :, cut], tfull.at[q, :, cut], f2_s.at[d], f2_r.at[d], x_peer[d])
-
-    for r in range(1, n_dp):
-        exchange(r).wait_recv()
-    for d in range(2):
-        share_first(d).start()
-
-    def give_back(away, c):
-        place = away * CORES + c
-        to = expert_at(away, c)
-        return copy(
-            rbuf.at[eight(place)], back.at[eight(e)], bs.at[place], br.at[back_from(away) * CORES + core], {"expert": to}
-        )
-
-    def add_up(far):
-        for h in range(2):
-            cut = cuts[far][h]
-            for d in range(2):
-                part_last(d, far, h).wait_recv()
-            total = pbuf[0, cut].astype(F32) + x2[0, cut].astype(F32) + x2[1, cut].astype(F32)
-            rbuf[cut, :] = total.astype(BF16)
-
-    def give(m, carry):
-        for c in range(CORES):
-            give_back(half_ring + m, c).start()
-            give_back(half_ring - 1 - m, c).start()
-        return carry
-
-    quarter_ring = half_ring // 2
+    hop(3)
+    pl.when(early)(share_forward)
+    own_half(2)
     add_up(0)
-    lax.fori_loop(0, quarter_ring, give, 0)
-    for d in range(2):
-        act_first(d).wait_recv()
-        act_second(d).start()
+    give_piece(0)
+    relay(2)
+    own_half(3)
+    act_forward(0)
     add_up(1)
-    lax.fori_loop(quarter_ring, half_ring - 1, give, 0)
-    for c in range(CORES):
-        give_back(chips - 1, c).start()
-    give_back(0, 1 - core).start()
-    kept = pltpu.make_async_copy(rbuf.at[eight(core)], back.at[eight(e)], bs.at[core])
+    give_piece(1)
+    relay(3)
+    pl.when(late)(share_start)
+    add_up(2)
+    give_piece(2)
+    act_forward(1)
+    add_up(3)
+    give_piece(3)
+    kept = pltpu.make_async_copy(rbuf.at[eight(e)], back.at[eight(e)], bs.at[e])
     kept.start()
-    for d in range(2):
-        share_first(d).wait_recv()
-        share_second(t_left if d == TO_RIGHT else t_right, d).start()
+    pl.when(late)(share_forward)
 
     for k in range(2):
         wsum[k] = nn(gact[3, k], rows_of(i, 0))
@@ -360,15 +392,14 @@
 
     for k in range(2):
         wsum[k] += nn(gact[0, k], group_rows(1)) + nn(gact[2, k], group_rows(3))
-    for d in range(2):
-        act_second(d).wait_recv()
     for k, out in enumerate((out_gate, out_up)):
+        for d in range(2):
+            act_second(k, d).wait_recv()
         out[...] = (wsum[k] + nn(gact[1, k], group_rows(2))).astype(BF16)
 
     def returned(away, c):
-        place = away * CORES + c
         source = expert_at(away, c)
-        copy(rbuf.at[eight(place)], back.at[eight(source)], bs.at[place], br.at[place], {"expert": other}).wait_recv()
+        copy(rbuf.at[eight(other)], back.at[eight(source)], bs.at[other], br.at[source], {"expert": other}).wait_recv()
 
     def take_back(away, carry):
         for c in range(CORES):
@@ -381,12 +412,12 @@
     out_rows[...] = tn(placer[...], back[...]).astype(BF16)
 
     dispatch(0, 1 - core).wait_send()
-    give_back(0, 1 - core).wait_send()
+    give_back(other).wait_send()
 
     def sent(away, carry):
         for c in range(CORES):
             dispatch(away, c).wait_send()
-            give_back(away, c).wait_send()
+            give_back(expert_at(away, c)).wait_send()
         return carry
 
     lax.fori_loop(1, chips, sent, 0)
@@ -401,17 +432,27 @@
     for r in range(1, n_dp):
         exchange(r).wait_send()
     for d in range(2):
-        act_first(d).wait_send()
-        act_second(d).wait_send()
+        for k in range(2):
+            act_first(k, d).wait_send()
+            act_second(k, d).wait_send()
         share_first(d).wait_send()
         share_second(t_left if d == TO_RIGHT else t_right, d).wait_send()
-        for far in range(2):
-            part_hop(d, far).wait_send()
+        for p in range(PIECES):
+            part_hop(d, p).wait_send()
             for h in range(2):
-                part_last(d, far, h).wait_send()
+                part_last(d, p, h).wait_send()
         for k in range(3):
             weight_first(k, d).wait_send()
             weight_second(k, d).wait_send()
+
+
+def write_out(*refs):
+    count = len(refs) // 2
+    copies = [pltpu.make_async_copy(refs[n], refs[count + n], refs[-1].at[n]) for n in range(count)]
+    for each in copies:
+        each.start()
+    for each in copies:
+        each.wait()
 
 
 def on_device(sizes, tokens, cotangent, expert_ids, gate_weight, up_weight, down_weight):
@@ -443,7 +484,7 @@
             pltpu.VMEM((n_tensor, n_dp - 1, rows, part // n_dp), BF16),
             pltpu.VMEM((2, hidden, depth), F32),
             pltpu.VMEM((n_tensor, rows, part), BF16),
-            pltpu.VMEM((2, 2, rows // 4, part), BF16),
+            pltpu.VMEM((2, PIECES, rows // 2 // PIECES, part), BF16),
             pltpu.VMEM((2, rows, part), BF16),
             pltpu.VMEM((rows, part), BF16),
             pltpu.VMEM((rows, part), BF16),
@@ -451,8 +492,8 @@
             dma((2, chips)), dma((2, chips)), dma((2, chips)), dma((2, chips)),
             dma((3, 2)), dma((3, 2)), dma((3, 2)), dma((3, 2)),
             dma((n_expert,)), dma((n_expert,)),
-            dma((2, 2)), dma((2, 2)), dma((2, 2, 2)), dma((2, 2, 2)),
-            dma((2,)), dma((2,)), dma((2,)), dma((2,)),
+            dma((2, PIECES)), dma((2, PIECES)), dma((2, PIECES, 2)), dma((2, PIECES, 2)),
+            dma((2, 2)), dma((2, 2)), dma((2, 2)), dma((2, 2)),
             dma((n_dp - 1,)), dma((n_dp - 1,)),
             dma((2,)), dma((2,)), dma((2,)), dma((2,)),
             pltpu.SemaphoreType.REGULAR((2,)),
@@ -462,6 +503,16 @@
         ),
         name="moe_backward",
     )(*(pltpu.with_memory_space_constraint(a, pltpu.HBM) for a in operands))
+    results = (grad_rows, grad_gate, grad_up)
+    grad_rows, grad_gate, grad_up = pl.pallas_call(
+        write_out,
+        out_shape=tuple(jax.ShapeDtypeStruct(r.shape, r.dtype) for r in results),
+        in_specs=[pl.BlockSpec(memory_space=pltpu.VMEM)] * 3,
+        out_specs=[pl.BlockSpec(memory_space=pltpu.HBM)] * 3,
+        scratch_shapes=[dma((3,))],
+        compiler_params=pltpu.CompilerParams(vmem_limit_bytes=32 << 20),
+        name="write_out",
+    )(*results)
     back = lambda g: jnp.swapaxes(g[None], 1, 2)
     return grad_rows, back(grad_gate), back(grad_up)
 

time: 82 us -> 79.2 us (0.966)
  local copies, waits for them, and re-layouts: 2.13 us -> 0 us
    unnamed x3 -> x0, local copies, waits for them, and re-layouts: 2.13 us -> none
    pallas_call x1, Pallas kernels: 79.1 us -> 77.5 us  [on_device(): pl.pallas_call(functools.partial(kernel, sizes), out_shape=(jax.ShapeDtyp...]
    pallas_call x0 -> x1, Pallas kernels: none -> 0.93 us  [on_device(): pl.pallas_call(write_out, out_shape=tuple((jax.ShapeDtypeStruct(r.shape,...]
where the time goes in v1:
time: 79.2 us; the launch traced here: 79.1 us
  Pallas kernels  78.4 us (99%)
    pallas_call x1, Pallas kernels, on_device(): pl.pallas_call(functools.partial(kernel, sizes), out_shape=(jax.ShapeDtyp...  77.5 us

profile of v1, /device:TPU:1, one launch (start us, length us, event | category | flops | bytes accessed | tf_op | source)
XLA Modules:
  0.0 79.1 jit_solution(12133712791697425094)
XLA Ops:
  0.6 77.5 %moe_backward.1 = (bf16[128,512]{1,0:T(8,128)(2,1)S(1)}, bf16[352,512]{1,0:T(8,128)(2,1)S(1)}, bf16[352,512]{1,0:T(8,128)(2,1)S(1)}) custom-call(s32[1,128]{1,0:T(1,128)} %bitcast.19, bf16[128,2048]{1,0:T(8,128)(2,1)} %tokens_hbm.1, bf16[128,2048]{1,0:T(8,128)(2,1)} %cotangent_hbm.1, bf16[352,512]{1,0:T(8,128)(2,1)} %bitcast.16, bf16[352,512]{1,0:T(8,128)(2,1)} %bitcast.17, ...), custom_call_target="tpu_custom_call" | custom-call | tf_op jit(solution)/shard_map/moe_backward/pallas_call | solution.py:466
  78.2 0.9 %write_out.1 = (bf16[128,512]{1,0:T(8,128)(2,1)}, bf16[352,512]{1,0:T(8,128)(2,1)}, bf16[352,512]{1,0:T(8,128)(2,1)}) custom-call(bf16[128,512]{1,0:T(8,128)(2,1)S(1)} %get-tuple-element.9.refs_0_, bf16[352,512]{1,0:T(8,128)(2,1)S(1)} %get-tuple-element.10.refs_1_, bf16[352,512]{1,0:T(8,128)(2,1)S(1)} %get-tuple-element.11.refs_2_), custom_call_target="tpu_custom_call" | custom-call | tf_op jit(solution)/shard_map/write_out/pallas_call | solution.py:507

commit v2 on v1

--- a/solution.py
+++ b/solution.py
@@ -10,7 +10,7 @@
 CAP = 8
 CORES = 2
 LAG = 4
-EARLY = 4
+EARLY = 8
 PIECES = 4
 F32 = jnp.float32
 BF16 = jnp.bfloat16
@@ -33,9 +33,9 @@
     sizes,
     ids_hbm, tokens_hbm, cotangent_hbm, gate_hbm, up_hbm, down_hbm,
     out_rows, out_gate, out_up,
-    ids, mine, sbuf, afull, wfull, placer, acc, gact, tfull, wsum, pbuf, x1, x2, rbuf, back,
-    ins, zs, zr, xg_s, xg_r, xh_s, xh_r, ws, wr, vs, vr, bs, br, p1_s, p1_r, p2_s, p2_r,
-    as_s, as_r, ah_s, ah_r, e_s, e_r, f1_s, f1_r, f2_s, f2_r, known,
+    ids, mine, sbuf, afull, wfull, placer, placer_t, acc, gact, tfull, wsum, pbuf, x1, x2, x3, rbuf, back,
+    ins, zs, zr, xg_s, xg_r, xh_s, xh_r, ws, wr, vs, vr, bs, br, p1_s, p1_r, p2_s, p2_r, p3_s, p3_r,
+    as_s, as_r, ah_s, ah_r, e_s, e_r, f1_s, f1_r, f2_s, f2_r, known, answer,
 ):
     n_dp, n_expert, n_tensor = sizes
     i, e, t = lax.axis_index("dp"), lax.axis_index("expert"), lax.axis_index("tensor")
@@ -63,11 +63,17 @@
     barrier = pltpu.get_barrier_semaphore()
     other = z * CORES + 1 - core
     z_next, z_prev = lax.rem(z + 1, chips), lax.rem(z + chips - 1, chips)
-    near = y_peer + x_peer + ({"dp": i_opp}, {"expert": other})
-    near += tuple({"expert": chip * CORES + c} for chip in (z_prev, z_next) for c in range(CORES))
+    near = y_peer + x_peer + ({"dp": i_opp}, {"tensor": t_opp}, {"expert": other})
+    last = z == chips - 1
+    ahead, behind = (tuple({"expert": chip * CORES + c} for c in range(CORES)) for chip in (z_next, z_prev))
     z_peer = ({"expert": z_prev * CORES + core}, {"expert": z_next * CORES + core})
-    for peer in near:
+    for peer in near + behind:
         pl.semaphore_signal(barrier, inc=1, device_id=peer, device_id_type=MESH)
+
+    @pl.when(z < chips - 1)
+    def _():
+        for peer in ahead:
+            pl.semaphore_signal(barrier, inc=1, device_id=peer, device_id_type=MESH)
 
     fetch_rows = [pltpu.make_async_copy(ids_hbm, ids, ins.at[0])]
     for kind, array in enumerate((tokens_hbm, cotangent_hbm)):
@@ -96,13 +102,29 @@
             weight_first(k, d).wait_recv()
             weight_second(k, d).start()
 
-    pl.semaphore_wait(barrier, len(near))
+    @pl.when(z > 0)
+    def _():
+        pl.semaphore_wait(barrier, len(near) + 2 * CORES)
+
+    @pl.when(z == 0)
+    def _():
+        pl.semaphore_wait(barrier, len(near) + CORES)
+
+    @pl.when(last)
+    def _():
+        for peer in ahead:
+            pl.semaphore_signal(answer.at[0], inc=1, device_id=peer, device_id_type=MESH)
+
     for k in range(3):
         for d in range(2):
             weight_first(k, d).start()
 
     def report(d):
         pl.semaphore_signal(known.at[d], inc=1, device_id=z_peer[d], device_id_type=MESH)
+
+    @pl.when(z == 0)
+    def _():
+        pl.semaphore_wait(answer.at[0], CORES)
 
     report(0)
     report(1)
@@ -226,8 +248,8 @@
             share_first(d).wait_recv()
             share_second(t_left if d == TO_RIGHT else t_right, d).start()
 
-    early = z < chips // EARLY
-    late = z >= chips // EARLY
+    early = z < 3 * chips // EARLY
+    late = z >= 3 * chips // EARLY
 
     own.wait()
     arrived(other)
@@ -312,6 +334,9 @@
         r = 1 if d == TO_RIGHT else 3
         return copy(pbuf.at[r, cut], x2.at[d, cut], p2_s.at[d, p, h], p2_r.at[d, p, h], x_peer[d])
 
+    def part_far(h):
+        return copy(pbuf.at[2, cuts[0][h]], x3.at[h], p3_s.at[h], p3_r.at[h], {"tensor": t_opp})
+
     def hop(p):
         for d in range(2):
             part_hop(d, p).start()
@@ -336,6 +361,9 @@
             for d in range(2):
                 part_last(d, p, h).wait_recv()
             total = pbuf[0, cut].astype(F32) + x2[0, cut].astype(F32) + x2[1, cut].astype(F32)
+            if p == 0:
+                part_far(h).wait_recv()
+                total += x3[h].astype(F32)
             rbuf[cut, :] = total.astype(BF16)
 
     def give(place):
@@ -351,21 +379,23 @@
             give(place)
 
     input_term(2)
-    hop(0)
+    for h in range(2):
+        part_far(h).start()
     hop(1)
     input_term(1)
     input_term(3)
-    own_half(0)
-    relay(0)
-    hop(2)
+    for h in range(2):
+        for d in range(2):
+            part_last(d, 0, h).start()
     own_half(1)
     input_term(0)
+    hop(2)
     relay(1)
+    add_up(0)
+    give_piece(0)
+    own_half(2)
     hop(3)
     pl.when(early)(share_forward)
-    own_half(2)
-    add_up(0)
-    give_piece(0)
     relay(2)
     own_half(3)
     act_forward(0)
@@ -406,10 +436,11 @@
             returned(away, c)
         return carry
 
+    placer_t[...] = placer[...].astype(F32).T.astype(BF16)
     kept.wait()
     returned(0, 1 - core)
     lax.fori_loop(1, chips, take_back, 0)
-    out_rows[...] = tn(placer[...], back[...]).astype(BF16)
+    out_rows[...] = nn(placer_t[...], back[...]).astype(BF16)
 
     dispatch(0, 1 - core).wait_send()
     give_back(other).wait_send()
@@ -437,8 +468,10 @@
             act_second(k, d).wait_send()
         share_first(d).wait_send()
         share_second(t_left if d == TO_RIGHT else t_right, d).wait_send()
+        part_far(d).wait_send()
         for p in range(PIECES):
-            part_hop(d, p).wait_send()
+            if p > 0:
+                part_hop(d, p).wait_send()
             for h in range(2):
                 part_last(d, p, h).wait_send()
         for k in range(3):
@@ -479,6 +512,7 @@
             pltpu.VMEM((n_tensor, rows, 2 * part), BF16),
             pltpu.VMEM((3, n_dp, hidden, depth), BF16),
             pltpu.VMEM((rows, block), BF16),
+            pltpu.VMEM((block, rows), BF16),
             pltpu.VMEM((3, hidden, rows), F32),
             pltpu.VMEM((n_dp, 2, hidden, rows), BF16),
             pltpu.VMEM((n_tensor, n_dp - 1, rows, part // n_dp), BF16),
@@ -486,17 +520,19 @@
             pltpu.VMEM((n_tensor, rows, part), BF16),
             pltpu.VMEM((2, PIECES, rows // 2 // PIECES, part), BF16),
             pltpu.VMEM((2, rows, part), BF16),
+            pltpu.VMEM((2, rows // 2 // PIECES, part), BF16),
             pltpu.VMEM((rows, part), BF16),
             pltpu.VMEM((rows, part), BF16),
             dma((1 + 2 * n_dp + 3,)), dma((n_expert,)), dma((n_expert,)),
             dma((2, chips)), dma((2, chips)), dma((2, chips)), dma((2, chips)),
             dma((3, 2)), dma((3, 2)), dma((3, 2)), dma((3, 2)),
             dma((n_expert,)), dma((n_expert,)),
-            dma((2, PIECES)), dma((2, PIECES)), dma((2, PIECES, 2)), dma((2, PIECES, 2)),
+            dma((2, PIECES)), dma((2, PIECES)), dma((2, PIECES, 2)), dma((2, PIECES, 2)), dma((2,)), dma((2,)),
             dma((2, 2)), dma((2, 2)), dma((2, 2)), dma((2, 2)),
             dma((n_dp - 1,)), dma((n_dp - 1,)),
             dma((2,)), dma((2,)), dma((2,)), dma((2,)),
             pltpu.SemaphoreType.REGULAR((2,)),
+            pltpu.SemaphoreType.REGULAR((1,)),
         ],
         compiler_params=pltpu.CompilerParams(
             collective_id=0, has_side_effects=True, vmem_limit_bytes=48 << 20

time: 79.2 us -> 77.6 us (0.980)
  Pallas kernels: 78.4 us -> 76.3 us
    pallas_call x1, Pallas kernels: 77.5 us -> 75.4 us  [on_device(): pl.pallas_call(functools.partial(kernel, sizes), out_shape=(jax.ShapeDtyp...]
where the time goes in v2:
time: 77.6 us; the launch traced here: 77 us
  Pallas kernels  76.3 us (98%)
    pallas_call x1, Pallas kernels, on_device(): pl.pallas_call(functools.partial(kernel, sizes), out_shape=(jax.ShapeDtyp...  75.4 us

profile of v2, /device:TPU:1, one launch (start us, length us, event | category | flops | bytes accessed | tf_op | source)
XLA Modules:
  0.0 77.0 jit_solution(4331468793630360552)
XLA Ops:
  0.6 75.4 %moe_backward.1 = (bf16[128,512]{1,0:T(8,128)(2,1)S(1)}, bf16[352,512]{1,0:T(8,128)(2,1)S(1)}, bf16[352,512]{1,0:T(8,128)(2,1)S(1)}) custom-call(s32[1,128]{1,0:T(1,128)} %bitcast.19, bf16[128,2048]{1,0:T(8,128)(2,1)} %tokens_hbm.1, bf16[128,2048]{1,0:T(8,128)(2,1)} %cotangent_hbm.1, bf16[352,512]{1,0:T(8,128)(2,1)} %bitcast.16, bf16[352,512]{1,0:T(8,128)(2,1)} %bitcast.17, ...), custom_call_target="tpu_custom_call" | custom-call | tf_op jit(solution)/shard_map/moe_backward/pallas_call | solution.py:499
  76.0 0.9 %write_out.1 = (bf16[128,512]{1,0:T(8,128)(2,1)}, bf16[352,512]{1,0:T(8,128)(2,1)}, bf16[352,512]{1,0:T(8,128)(2,1)}) custom-call(bf16[128,512]{1,0:T(8,128)(2,1)S(1)} %get-tuple-element.9.refs_0_, bf16[352,512]{1,0:T(8,128)(2,1)S(1)} %get-tuple-element.10.refs_1_, bf16[352,512]{1,0:T(8,128)(2,1)S(1)} %get-tuple-element.11.refs_2_), custom_call_target="tpu_custom_call" | custom-call | tf_op jit(solution)/shard_map/write_out/pallas_call | solution.py:543

commit v3 on v2

--- a/solution.py
+++ b/solution.py
@@ -10,7 +10,7 @@
 CAP = 8
 CORES = 2
 LAG = 4
-EARLY = 8
+
 PIECES = 4
 F32 = jnp.float32
 BF16 = jnp.bfloat16
@@ -248,8 +248,8 @@
             share_first(d).wait_recv()
             share_second(t_left if d == TO_RIGHT else t_right, d).start()
 
-    early = z < 3 * chips // EARLY
-    late = z >= 3 * chips // EARLY
+    early = z < chips // 2
+    late = z >= chips // 2
 
     own.wait()
     arrived(other)

time: 77.6 us -> 77.2 us (level)
  no operation moved by 1% of the time
where the time goes in v3:
time: 77.2 us; the launch traced here: 76.3 us
  Pallas kernels  75.7 us (98%)
    pallas_call x1, Pallas kernels, on_device(): pl.pallas_call(functools.partial(kernel, sizes), out_shape=(jax.ShapeDtyp...  74.8 us

profile of v3, /device:TPU:1, one launch (start us, length us, event | category | flops | bytes accessed | tf_op | source)
XLA Modules:
  0.0 76.3 jit_solution(17244692086574612741)
XLA Ops:
  0.6 74.8 %moe_backward.1 = (bf16[128,512]{1,0:T(8,128)(2,1)S(1)}, bf16[352,512]{1,0:T(8,128)(2,1)S(1)}, bf16[352,512]{1,0:T(8,128)(2,1)S(1)}) custom-call(s32[1,128]{1,0:T(1,128)} %bitcast.19, bf16[128,2048]{1,0:T(8,128)(2,1)} %tokens_hbm.1, bf16[128,2048]{1,0:T(8,128)(2,1)} %cotangent_hbm.1, bf16[352,512]{1,0:T(8,128)(2,1)} %bitcast.16, bf16[352,512]{1,0:T(8,128)(2,1)} %bitcast.17, ...), custom_call_target="tpu_custom_call" | custom-call | tf_op jit(solution)/shard_map/moe_backward/pallas_call | solution.py:499
  75.4 0.9 %write_out.1 = (bf16[128,512]{1,0:T(8,128)(2,1)}, bf16[352,512]{1,0:T(8,128)(2,1)}, bf16[352,512]{1,0:T(8,128)(2,1)}) custom-call(bf16[128,512]{1,0:T(8,128)(2,1)S(1)} %get-tuple-element.9.refs_0_, bf16[352,512]{1,0:T(8,128)(2,1)S(1)} %get-tuple-element.10.refs_1_, bf16[352,512]{1,0:T(8,128)(2,1)S(1)} %get-tuple-element.11.refs_2_), custom_call_target="tpu_custom_call" | custom-call | tf_op jit(solution)/shard_map/write_out/pallas_call | solution.py:543
